TPU v7x, 32 devices: a whole 2x2x4 slice. The times are simulated.
32 devices in a mesh: grp: 2 (over x), con: 16 (over z, y, core).
Axes of the slice: x: 2, y: 2, z: 4, core: 2. Of those that a mesh axis runs over, the one named last changes fastest.
Arguments:
- matrix: float32 [32768, 2048], P(('grp', 'con')), parts along dimension 0, may hold values from -0.046875 to 0.046875
- bounds_rhs: float32 [32768, 128], P(('grp', 'con')), parts along dimension 0, may hold values from -3 to 3
- costs: float32 [4096, 128], P(('grp', 'con')), parts along dimension 0, may hold values from -12 to 12
- upper: float32 [4096], P(('grp', 'con')), parts along dimension 0, may hold values from 0.5 to 2
- bound_mask: int32 [4096], P(('grp', 'con')), parts along dimension 0, may hold values 0 or 1
- node_map: int32 [3, 256], P(None, 'grp'), parts along dimension 1, may hold values from 0 to 63, as said below
- weights: int32 [256], P('grp'), parts along dimension 0, may hold values from 1 to 10
Outputs:
- primal: float32 [4096, 128], P(('grp', 'con')), parts along dimension 0
- dual: float32 [32768, 128], P(('grp', 'con')), parts along dimension 0
- multipliers: float32 [4096, 128], P(('grp', 'con')), parts along dimension 0
- gaps: float32 [4], P('grp'), parts along dimension 0
There are 2 independent parts, one for each index of `grp`. A program takes and returns all parts, laid end to end along the dimension named above; each array names one. Nothing has to cross between parts.
Inputs may be any that keep to these rules, and one draw needn't show every extreme that they name: `node_map`: row t numbers the 4 ** (t + 1) nodes of that section; each node holds 128 / 4 ** (t + 1) scenarios, and the nodes of row t + 1 split those of row t.
All inputs are finite; a program needn't handle non-finite values. No bound on the sum of `bound_mask` on one device may be relied on, other than what follows from the above.
Results may differ from a plain program's by a relative error of at most 0.0001.
Values sent between devices are 32-bit elements; how exact they have to be, the bound alone decides.
A program may use at most 64 MiB of HBM per device.

v0:
```python
import jax
import jax.numpy as jnp
from jax import lax
from jax.sharding import PartitionSpec as P

N = 2048
OUTER = 2
INNER = 2
highest = lax.Precision.HIGHEST
step_primal = 0.4
step_dual = 0.6
penalty = 1.0


def node_average(node_map, weights):
    weight_float = weights.astype(jnp.float32)
    probability = weight_float / jnp.sum(weight_float)
    same_node = (node_map[:, :, None] == node_map[:, None, :]).astype(jnp.float32)
    node_mass = same_node * probability[None, None, :]
    return (node_mass / jnp.sum(node_mass, axis=2, keepdims=True), probability)


def consensus(primal, averaging, column_index):
    averaged = jnp.einsum("tsr,jr->tjs", averaging, primal, precision=highest)
    section_of = column_index % (averaging.shape[0] + 1)
    section_hot = (
        section_of[None, :] == jnp.arange(averaging.shape[0], dtype=jnp.int32)[:, None]
    ).astype(jnp.float32)
    free_cols = 1.0 - jnp.sum(section_hot, axis=0)
    return jnp.sum(section_hot[:, :, None] * averaged, axis=0) + free_cols[:, None] * primal


def primal_step(primal, costs, multipliers, average, transposed, upper, flags, prox_weight):
    gradient = costs + multipliers + prox_weight * (primal - average) + transposed
    moved = jnp.maximum(primal - step_primal * gradient, 0.0)
    return jnp.where(flags[:, None] > 0, jnp.minimum(moved, upper[:, None]), moved)


def apply_rows(matrix, extrap):
    return jnp.dot(matrix, lax.all_gather(extrap, "con", axis=0, tiled=True), precision=highest)


def apply_columns(matrix, dual):
    return lax.psum_scatter(
        lax.dot_general(matrix, dual, (((0,), (0,)), ((), ())), precision=highest),
        "con",
        scatter_dimension=0,
        tiled=True,
    )


def body(matrix, bounds_rhs, costs, upper, bound_mask, node_map, weights):
    own_cols = costs.shape[0]
    scenario_count = costs.shape[1]
    averaging, probability = node_average(node_map, weights)
    start_col = lax.axis_index("con") * own_cols
    costs_all, upper_all, flags_all = (costs, upper, bound_mask.astype(jnp.float32))
    width = costs_all.shape[0]
    column_index = start_col + jnp.arange(width, dtype=jnp.int32)
    primal = jnp.zeros((width, scenario_count), jnp.float32)
    multipliers = jnp.zeros((width, scenario_count), jnp.float32)
    average = jnp.zeros((width, scenario_count), jnp.float32)
    transposed = jnp.zeros((width, scenario_count), jnp.float32)
    dual = jnp.zeros(bounds_rhs.shape, jnp.float32)
    partials = []
    for outer_turn in range(OUTER):
        prox_weight = 0.0 if outer_turn == 0 else penalty
        for inner_turn in range(INNER):
            moved = primal_step(
                primal,
                costs_all,
                multipliers,
                average,
                transposed,
                upper_all,
                flags_all,
                prox_weight,
            )
            extrap = 2.0 * moved - primal
            product = apply_rows(matrix, extrap)
            dual = jnp.maximum(dual + step_dual * (product - bounds_rhs), 0.0)
            primal = moved
            if outer_turn < OUTER - 1 or inner_turn < INNER - 1:
                transposed = apply_columns(matrix, dual)
        average = consensus(primal, averaging, column_index)
        deviation = primal - average
        multipliers = multipliers + penalty * deviation
        partial_value = jnp.sum(deviation * deviation * probability[None, :]) / N
        partial_value = lax.psum(partial_value, "con")
        partials.append(partial_value)
    gaps = jnp.stack(partials)
    return (primal, dual, multipliers, gaps)


def solution(mesh):
    placed = (
        P(("grp", "con"), None),
        P(("grp", "con"), None),
        P(("grp", "con"), None),
        P(("grp", "con")),
        P(("grp", "con")),
        P(None, "grp"),
        P("grp"),
    )
    return jax.shard_map(
        body,
        mesh=mesh,
        in_specs=placed,
        out_specs=(
            P(("grp", "con"), None),
            P(("grp", "con"), None),
            P(("grp", "con"), None),
            P("grp"),
        ),
        check_vma=False,
    )
```

profile of v0, /device:TPU:0, one launch (start us, length us, event | category | flops | bytes accessed | tf_op | source)
XLA Modules:
  0.0 413.3 jit_solution(4604648816111772595)
XLA Ops:
  7.9 0.9 copy.23
  8.8 1.3 fusion.31
  10.2 1.2 copy.25
  11.4 38.8 %all-gather.5.cloned.1.call-done = f32[2048,128]{0,1:T(8,128)} async-done(((f32[128,128]{0,1:T(8,128)}), f32[2048,128]{0,1:T(8,128)}) %all-gather.5.cloned.1.call-update) | async-done | bytes 1048592 | tf_op jit(solution)/shard_map/all_gather | solution.py:40
  50.3 12.0 %fusion.8 = f32[1024,128]{0,1:T(8,128)S(1)} fusion(f32[1024,128]{0,1:T(8,128)S(1)} %copy.25, f32[2048,128]{0,1:T(8,128)} %all-gather.5.cloned.1.call-done, f32[1024,2048]{1,0:T(8,128)} %param.7), kind=kOutput, calls=%fused_computation.15 | convolution fusion | flops 3221618688 | bytes 10485760 | tf_op jit(solution)/shard_map/dot_general | solution.py:40
  62.3 5.6 %convolution_bitcast_fusion.2 = f32[2048,128]{0,1:T(8,128)} fusion(f32[1024,128]{0,1:T(8,128)S(1)} %fusion.8, f32[1024,2048]{1,0:T(8,128)S(1)} %copy-done), kind=kOutput, calls=%fused_computation.2 | convolution fusion | flops 3221225472 | bytes 9961472 | tf_op jit(solution)/shard_map/dot_general | solution.py:45
  67.9 57.0 %reduce-scatter.4.cloned.1.call-done = f32[128,128]{0,1:T(8,128)} async-done(((f32[2048,128]{0,1:T(8,128)}), f32[128,128]{0,1:T(8,128)}) %reduce-scatter.4.cloned.1.call-update) | async-done | bytes 65552 | tf_op jit(solution)/shard_map/reduce_scatter | solution.py:44
  124.9 1.5 multiply_subtract_fusion.2
  126.7 37.0 %all-gather.7.cloned.1.call-done = f32[2048,128]{0,1:T(8,128)} async-done(((f32[128,128]{0,1:T(8,128)}), f32[2048,128]{0,1:T(8,128)}) %all-gather.7.cloned.1.call-update) | async-done | bytes 1048592 | tf_op jit(solution)/shard_map/all_gather | solution.py:40
  163.7 11.5 %fusion.10 = f32[1024,128]{0,1:T(8,128)S(1)} fusion(f32[1024,128]{0,1:T(8,128)S(1)} %fusion.8, f32[1024,128]{0,1:T(8,128)S(1)} %copy.25, f32[2048,128]{0,1:T(8,128)} %all-gather.7.cloned.1.call-done, f32[1024,2048]{1,0:T(8,128)} %param.7), kind=kOutput, calls=%fused_computation.17 | convolution fusion | flops 3221749760 | bytes 11010048 | tf_op jit(solution)/shard_map/dot_general | solution.py:40
  175.2 7.8 %convolution_bitcast_fusion.1 = f32[2048,128]{0,1:T(8,128)} fusion(f32[1024,128]{0,1:T(8,128)S(1)} %fusion.10, f32[1024,2048]{1,0:T(8,128)} %param.7), kind=kOutput, calls=%fused_computation.1 | convolution fusion | flops 3221225472 | bytes 9961472 | tf_op jit(solution)/shard_map/dot_general | solution.py:45
  185.3 54.8 %reduce-scatter.6.cloned.1.call-done = f32[128,128]{0,1:T(8,128)} async-done(((f32[2048,128]{0,1:T(8,128)}), f32[128,128]{0,1:T(8,128)}) %reduce-scatter.6.cloned.1.call-update) | async-done | bytes 65552 | tf_op jit(solution)/shard_map/reduce_scatter | solution.py:44
  240.1 1.5 multiply_subtract_fusion.1
  241.9 36.7 %all-gather.9.cloned.1.call-done = f32[2048,128]{0,1:T(8,128)} async-done(((f32[128,128]{0,1:T(8,128)}), f32[2048,128]{0,1:T(8,128)}) %all-gather.9.cloned.1.call-update) | async-done | bytes 1048592 | tf_op jit(solution)/shard_map/all_gather | solution.py:40
  278.6 11.4 %fusion.12 = f32[1024,128]{0,1:T(8,128)S(1)} fusion(f32[1024,128]{0,1:T(8,128)S(1)} %fusion.10, f32[1024,128]{0,1:T(8,128)S(1)} %copy.25, f32[2048,128]{0,1:T(8,128)} %all-gather.9.cloned.1.call-done, f32[1024,2048]{1,0:T(8,128)} %param.7), kind=kOutput, calls=%fused_computation.19 | convolution fusion | flops 3221749760 | bytes 11010048 | tf_op jit(solution)/shard_map/dot_general | solution.py:40
  290.0 7.8 %convolution_bitcast_fusion = f32[2048,128]{0,1:T(8,128)} fusion(f32[1024,128]{0,1:T(8,128)S(1)} %fusion.12, f32[1024,2048]{1,0:T(8,128)} %param.7), kind=kOutput, calls=%fused_computation | convolution fusion | flops 3221225472 | bytes 9961472 | tf_op jit(solution)/shard_map/dot_general | solution.py:45
  297.9 57.0 %reduce-scatter.8.cloned.1.call-done = f32[128,128]{0,1:T(8,128)} async-done(((f32[2048,128]{0,1:T(8,128)}), f32[128,128]{0,1:T(8,128)}) %reduce-scatter.8.cloned.1.call-update) | async-done | bytes 65552 | tf_op jit(solution)/shard_map/reduce_scatter | solution.py:44
  355.0 1.5 multiply_subtract_fusion
  359.1 31.6 %all-reduce = (f32[1]{0:T(128)}, f32[1]{0:T(128)}) all-reduce(f32[1]{0:T(128)} %bitcast.12, f32[1]{0:T(128)} %bitcast.11), channel_id=1, replica_groups=mesh['grp'=2,'con'=16] {'con'}, use_global_device_ids=true, to_apply=%region_11.12 | all-reduce | flops 2 | bytes 16 | tf_op jit(solution)/shard_map/psum | solution.py:89
  390.7 0.7 copy.34
  391.4 0.7 copy.36
  392.2 1.8 pad_maximum_fusion
  394.0 11.5 %fusion.14 = f32[1024,128]{0,1:T(8,128)S(1)} fusion(f32[1024,128]{0,1:T(8,128)S(1)} %fusion.12, f32[1024,128]{0,1:T(8,128)S(1)} %copy.25, f32[2048,128]{0,1:T(8,128)} %all-gather.11.cloned.1.call-done, f32[1024,2048]{1,0:T(8,128)} %param.7), kind=kOutput, calls=%fused_computation.21 | convolution fusion | flops 3221749760 | bytes 11010048 | tf_op jit(solution)/shard_map/dot_general | solution.py:40
  405.5 1.0 copy.35
  (36 shorter events, 4.9 us)
Async XLA Ops:
  7.2 43.1 %all-gather.5.cloned.1.call-start = ((), (), s32[]{:S(2)}) async-start(), calls=%async_computation.3 | async-start | bytes 1114112 | tf_op jit(solution)/shard_map/all_gather | solution.py:40
  10.1 114.8 %reduce-scatter.4.cloned.1.call-start = ((), (), s32[]{:S(2)}) async-start(), calls=%async_computation.4 | async-start | bytes 1114112 | tf_op jit(solution)/shard_map/reduce_scatter | solution.py:44
  11.4 113.5 %copy-start.2 = (f32[128]{0:T(128)S(1)}, f32[128]{0:T(128)}, u32[]{:S(2)}) copy-start(f32[128]{0:T(128)} %param.10) | copy-start | bytes 1540
  50.3 12.0 %copy-start = (f32[1024,2048]{1,0:T(8,128)S(1)}, f32[1024,2048]{1,0:T(8,128)}, u32[]{:S(2)}) copy-start(f32[1024,2048]{1,0:T(8,128)} %param.7) | copy-start | bytes 25165828
  67.9 95.9 %all-gather.7.cloned.1.call-start = ((), (), s32[]{:S(2)}) async-start(), calls=%async_computation.5 | async-start | bytes 1114112 | tf_op jit(solution)/shard_map/all_gather | solution.py:40
  126.5 56.7 %copy-start.3 = (s32[128]{0:T(128)S(1)}, s32[128]{0:T(128)}, u32[]{:S(2)}) copy-start(s32[128]{0:T(128)} %param.13) | copy-start | bytes 1540
  126.5 57.9 %copy-start.1 = (s32[3,128]{1,0:T(4,128)S(1)}, s32[3,128]{1,0:T(4,128)}, u32[]{:S(2)}) copy-start(s32[3,128]{1,0:T(4,128)} %param.12) | copy-start | bytes 4612
  126.5 113.6 %reduce-scatter.6.cloned.1.call-start = ((), (), s32[]{:S(2)}) async-start(), calls=%async_computation.6 | async-start | bytes 1114112 | tf_op jit(solution)/shard_map/reduce_scatter | solution.py:44
  183.1 95.5 %all-gather.9.cloned.1.call-start = ((), (), s32[]{:S(2)}) async-start(), calls=%async_computation.7 | async-start | bytes 1114112 | tf_op jit(solution)/shard_map/all_gather | solution.py:40
  241.6 113.4 %reduce-scatter.8.cloned.1.call-start = ((), (), s32[]{:S(2)}) async-start(), calls=%async_computation.8 | async-start | bytes 1114112 | tf_op jit(solution)/shard_map/reduce_scatter | solution.py:44
  297.9 96.1 %all-gather.11.cloned.1.call-start = ((), (), s32[]{:S(2)}) async-start(), calls=%async_computation.9 | async-start | bytes 1114112 | tf_op jit(solution)/shard_map/all_gather | solution.py:40
Sparse Core Ops, SparseCore 0:
  10.7 39.4 all-gather.4
  68.0 56.8 reduce-scatter.3
  127.9 35.7 all-gather.6
  183.2 56.8 reduce-scatter.5
  242.7 35.8 all-gather.8
  298.0 56.9 reduce-scatter.7
  357.9 35.7 all-gather.10
where the time goes:
time: 414 us; the launch traced here: 413 us
  waiting for transfers between devices  281 us (68%)
  matrix products  68.6 us (17%)
  blocking collectives  31.6 us (8%)
  between operations  15.6 us (4%)
  other arithmetic  10.5 us (3%)
  local copies, waits for them, and re-layouts  4.82 us (1%)
    reduce_scatter x3, waiting for transfers between devices, apply_columns(): lax.psum_scatter(lax.dot_general(matrix, dual, (((0,), (0,)), ((), ())),...  169 us
    all_gather x4, waiting for transfers between devices, apply_rows(): lax.all_gather(extrap, 'con', axis=0, tiled=True)  112 us
    dot_general x4, matrix products, apply_rows(): jnp.dot(matrix, lax.all_gather(extrap, 'con', axis=0, tiled=True), precis...  46.3 us
    psum x1, blocking collectives, body(): partial_value = lax.psum(partial_value, 'con')  31.6 us
    dot_general x3, matrix products, apply_columns(): lax.dot_general(matrix, dual, (((0,), (0,)), ((), ())), precision=highest)  21.3 us
  transfers between devices with their start and end apart: 7, of which 6 were waited for; matrix products, arithmetic and copies ran while one was open for 2% of the time, Pallas kernels for 0%

commit v1 on v0

--- a/solution.py
+++ b/solution.py
@@ -86,7 +86,15 @@
         deviation = primal - average
         multipliers = multipliers + penalty * deviation
         partial_value = jnp.sum(deviation * deviation * probability[None, :]) / N
-        partial_value = lax.psum(partial_value, "con")
+        cores_n = jax.lax.psum(1, axis_name="con")
+        earlier, left_arr = (partial_value, 0)
+        while 1 << left_arr < cores_n:
+            r1 = jax.lax.ppermute(
+                earlier, axis_name="con", perm=[(b, b ^ 1 << left_arr) for b in range(cores_n)]
+            )
+            earlier = earlier + r1
+            left_arr = left_arr + 1
+        partial_value = earlier
         partials.append(partial_value)
     gaps = jnp.stack(partials)
     return (primal, dual, multipliers, gaps)

time: 414 us -> 413 us (level)
  blocking collectives: 31.6 us -> 0 us
  starting transfers between devices: 0.69 us -> 18.1 us
  waiting for transfers between devices: 281 us -> 292 us
  between operations: 15.6 us -> 20.6 us
    psum x1 -> x0, blocking collectives: 31.6 us -> none  [body(): partial_value = lax.psum(partial_value, 'con')]
    ppermute x0 -> x8, starting transfers between devices: none -> 17.4 us  [body(): jax.lax.ppermute(earlier, axis_name='con', perm=[(b, b ^ 1 << left_arr) f...]
    all_gather x4, waiting for transfers between devices: 112 us -> 122 us  [apply_rows(): lax.all_gather(extrap, 'con', axis=0, tiled=True)]
  transfers between devices with their start and end apart: 7 -> 15, of which waited for: 6 -> 8; matrix products, arithmetic and copies ran while one was open for 2% -> 2% of each run, Pallas kernels for 0% -> 0%
where the time goes in v1:
time: 413 us
  waiting for transfers between devices  292 us (71%)
  matrix products  68.6 us (17%)
  between operations  20.6 us (5%)
  starting transfers between devices  18.1 us (4%)
  other arithmetic  9.27 us (2%)
  local copies, waits for them, and re-layouts  4.82 us (1%)
    reduce_scatter x3, waiting for transfers between devices, apply_columns(): lax.psum_scatter(lax.dot_general(matrix, dual, (((0,), (0,)), ((), ())),...  169 us
    all_gather x4, waiting for transfers between devices, apply_rows(): lax.all_gather(extrap, 'con', axis=0, tiled=True)  122 us
    dot_general x4, matrix products, apply_rows(): jnp.dot(matrix, lax.all_gather(extrap, 'con', axis=0, tiled=True), precis...  46.4 us
    dot_general x3, matrix products, apply_columns(): lax.dot_general(matrix, dual, (((0,), (0,)), ((), ())), precision=highest)  21.2 us
    ppermute x8, starting transfers between devices, body(): jax.lax.ppermute(earlier, axis_name='con', perm=[(b, b ^ 1 << left_arr) f...  17.4 us
  transfers between devices with their start and end apart: 15, of which 8 were waited for; matrix products, arithmetic and copies ran while one was open for 2% of the time, Pallas kernels for 0%

profile of v1, /device:TPU:0, one launch (start us, length us, event | category | flops | bytes accessed | tf_op | source)
XLA Modules:
  0.0 413.0 jit_solution(10648010877519822180)
XLA Ops:
  11.4 38.8 %all-gather.5.cloned.1.call-done = f32[2048,128]{0,1:T(8,128)} async-done(((f32[128,128]{0,1:T(8,128)}), f32[2048,128]{0,1:T(8,128)}) %all-gather.5.cloned.1.call-update) | async-done | bytes 1048592 | tf_op jit(solution)/shard_map/all_gather | solution.py:40
  50.3 12.0 %fusion.8 = f32[1024,128]{0,1:T(8,128)S(1)} fusion(f32[1024,128]{0,1:T(8,128)S(1)} %copy.25, f32[2048,128]{0,1:T(8,128)} %all-gather.5.cloned.1.call-done, f32[1024,2048]{1,0:T(8,128)} %param.7), kind=kOutput, calls=%fused_computation.15 | convolution fusion | flops 3221618688 | bytes 10485760 | tf_op jit(solution)/shard_map/dot_general | solution.py:40
  62.3 5.5 %convolution_bitcast_fusion.2 = f32[2048,128]{0,1:T(8,128)} fusion(f32[1024,128]{0,1:T(8,128)S(1)} %fusion.8, f32[1024,2048]{1,0:T(8,128)S(1)} %copy-done), kind=kOutput, calls=%fused_computation.2 | convolution fusion | flops 3221225472 | bytes 9961472 | tf_op jit(solution)/shard_map/dot_general | solution.py:45
  67.9 57.0 %reduce-scatter.4.cloned.1.call-done = f32[128,128]{0,1:T(8,128)} async-done(((f32[2048,128]{0,1:T(8,128)}), f32[128,128]{0,1:T(8,128)}) %reduce-scatter.4.cloned.1.call-update) | async-done | bytes 65552 | tf_op jit(solution)/shard_map/reduce_scatter | solution.py:44
  125.0 1.5 multiply_subtract_fusion.2
  126.7 37.0 %all-gather.7.cloned.1.call-done = f32[2048,128]{0,1:T(8,128)} async-done(((f32[128,128]{0,1:T(8,128)}), f32[2048,128]{0,1:T(8,128)}) %all-gather.7.cloned.1.call-update) | async-done | bytes 1048592 | tf_op jit(solution)/shard_map/all_gather | solution.py:40
  163.8 11.5 %fusion.10 = f32[1024,128]{0,1:T(8,128)S(1)} fusion(f32[1024,128]{0,1:T(8,128)S(1)} %fusion.8, f32[1024,128]{0,1:T(8,128)S(1)} %copy.25, f32[2048,128]{0,1:T(8,128)} %all-gather.7.cloned.1.call-done, f32[1024,2048]{1,0:T(8,128)} %param.7), kind=kOutput, calls=%fused_computation.17 | convolution fusion | flops 3221749760 | bytes 11010048 | tf_op jit(solution)/shard_map/dot_general | solution.py:40
  175.2 7.8 %convolution_bitcast_fusion.1 = f32[2048,128]{0,1:T(8,128)} fusion(f32[1024,128]{0,1:T(8,128)S(1)} %fusion.10, f32[1024,2048]{1,0:T(8,128)} %param.7), kind=kOutput, calls=%fused_computation.1 | convolution fusion | flops 3221225472 | bytes 9961472 | tf_op jit(solution)/shard_map/dot_general | solution.py:45
  185.3 54.8 %reduce-scatter.6.cloned.1.call-done = f32[128,128]{0,1:T(8,128)} async-done(((f32[2048,128]{0,1:T(8,128)}), f32[128,128]{0,1:T(8,128)}) %reduce-scatter.6.cloned.1.call-update) | async-done | bytes 65552 | tf_op jit(solution)/shard_map/reduce_scatter | solution.py:44
  240.1 1.5 multiply_subtract_fusion.1
  241.9 36.6 %all-gather.9.cloned.1.call-done = f32[2048,128]{0,1:T(8,128)} async-done(((f32[128,128]{0,1:T(8,128)}), f32[2048,128]{0,1:T(8,128)}) %all-gather.9.cloned.1.call-update) | async-done | bytes 1048592 | tf_op jit(solution)/shard_map/all_gather | solution.py:40
  278.5 11.5 %fusion.12 = f32[1024,128]{0,1:T(8,128)S(1)} fusion(f32[1024,128]{0,1:T(8,128)S(1)} %fusion.10, f32[1024,128]{0,1:T(8,128)S(1)} %copy.25, f32[2048,128]{0,1:T(8,128)} %all-gather.9.cloned.1.call-done, f32[1024,2048]{1,0:T(8,128)} %param.7), kind=kOutput, calls=%fused_computation.19 | convolution fusion | flops 3221749760 | bytes 11010048 | tf_op jit(solution)/shard_map/dot_general | solution.py:40
  290.0 7.8 %convolution_bitcast_fusion = f32[2048,128]{0,1:T(8,128)} fusion(f32[1024,128]{0,1:T(8,128)S(1)} %fusion.12, f32[1024,2048]{1,0:T(8,128)} %param.7), kind=kOutput, calls=%fused_computation | convolution fusion | flops 3221225472 | bytes 9961472 | tf_op jit(solution)/shard_map/dot_general | solution.py:45
  297.9 57.0 %reduce-scatter.8.cloned.1.call-done = f32[128,128]{0,1:T(8,128)} async-done(((f32[2048,128]{0,1:T(8,128)}), f32[128,128]{0,1:T(8,128)}) %reduce-scatter.8.cloned.1.call-update) | async-done | bytes 65552 | tf_op jit(solution)/shard_map/reduce_scatter | solution.py:44
  354.9 1.5 multiply_subtract_fusion
  361.3 1.5 collective-permute-start.4
  363.4 2.6 collective-permute-start.1
  366.7 2.1 collective-permute-start.5
  369.4 2.7 collective-permute-start.2
  372.7 2.1 collective-permute-start.6
  375.4 2.7 collective-permute-start.3
  378.8 2.9 collective-permute-start.7
  384.4 9.2 %all-gather.11.cloned.1.call-done = f32[2048,128]{0,1:T(8,128)} async-done(((f32[128,128]{0,1:T(8,128)}), f32[2048,128]{0,1:T(8,128)}) %all-gather.11.cloned.1.call-update) | async-done | bytes 1048592 | tf_op jit(solution)/shard_map/all_gather | solution.py:40
  393.7 11.5 %fusion.14 = f32[1024,128]{0,1:T(8,128)S(1)} fusion(f32[1024,128]{0,1:T(8,128)S(1)} %fusion.12, f32[1024,128]{0,1:T(8,128)S(1)} %copy.25, f32[2048,128]{0,1:T(8,128)} %all-gather.11.cloned.1.call-done, f32[1024,2048]{1,0:T(8,128)} %param.7), kind=kOutput, calls=%fused_computation.21 | convolution fusion | flops 3221749760 | bytes 11010048 | tf_op jit(solution)/shard_map/dot_general | solution.py:40
  (51 shorter events, 13.2 us)
Async XLA Ops:
  7.2 43.1 %all-gather.5.cloned.1.call-start = ((), (), s32[]{:S(2)}) async-start(), calls=%async_computation.3 | async-start | bytes 1114112 | tf_op jit(solution)/shard_map/all_gather | solution.py:40
  10.1 114.8 %reduce-scatter.4.cloned.1.call-start = ((), (), s32[]{:S(2)}) async-start(), calls=%async_computation.4 | async-start | bytes 1114112 | tf_op jit(solution)/shard_map/reduce_scatter | solution.py:44
  11.4 113.5 %copy-start.2 = (f32[128]{0:T(128)S(1)}, f32[128]{0:T(128)}, u32[]{:S(2)}) copy-start(f32[128]{0:T(128)} %param.10) | copy-start | bytes 1540
  50.3 12.0 %copy-start = (f32[1024,2048]{1,0:T(8,128)S(1)}, f32[1024,2048]{1,0:T(8,128)}, u32[]{:S(2)}) copy-start(f32[1024,2048]{1,0:T(8,128)} %param.7) | copy-start | bytes 25165828
  67.9 95.9 %all-gather.7.cloned.1.call-start = ((), (), s32[]{:S(2)}) async-start(), calls=%async_computation.5 | async-start | bytes 1114112 | tf_op jit(solution)/shard_map/all_gather | solution.py:40
  126.5 56.7 %copy-start.3 = (s32[128]{0:T(128)S(1)}, s32[128]{0:T(128)}, u32[]{:S(2)}) copy-start(s32[128]{0:T(128)} %param.13) | copy-start | bytes 1540
  126.5 57.9 %copy-start.1 = (s32[3,128]{1,0:T(4,128)S(1)}, s32[3,128]{1,0:T(4,128)}, u32[]{:S(2)}) copy-start(s32[3,128]{1,0:T(4,128)} %param.12) | copy-start | bytes 4612
  126.5 113.6 %reduce-scatter.6.cloned.1.call-start = ((), (), s32[]{:S(2)}) async-start(), calls=%async_computation.6 | async-start | bytes 1114112 | tf_op jit(solution)/shard_map/reduce_scatter | solution.py:44
  183.1 95.5 %all-gather.9.cloned.1.call-start = ((), (), s32[]{:S(2)}) async-start(), calls=%async_computation.7 | async-start | bytes 1114112 | tf_op jit(solution)/shard_map/all_gather | solution.py:40
  241.7 113.2 %reduce-scatter.8.cloned.1.call-start = ((), (), s32[]{:S(2)}) async-start(), calls=%async_computation.8 | async-start | bytes 1114112 | tf_op jit(solution)/shard_map/reduce_scatter | solution.py:44
  297.8 95.8 %all-gather.11.cloned.1.call-start = ((), (), s32[]{:S(2)}) async-start(), calls=%async_computation.9 | async-start | bytes 1114112 | tf_op jit(solution)/shard_map/all_gather | solution.py:40
  360.5 2.3 collective-permute-start
  361.3 4.7 %collective-permute-start.4 = (f32[]{:T(128)}, f32[]{:T(128)}, u32[]{:S(2)}, u32[]{:S(2)}) collective-permute-start(f32[]{:T(128)} %div.25), channel_id=1, source_target_pairs={{0,1},{1,0},{2,3},{3,2},{4,5},{5,4},{6,7},{7,6},{8,9},{9,8},{10,11... | collective-permute-start | bytes 20 | tf_op jit(solution)/shard_map/ppermute | solution.py:92
  363.4 5.4 %collective-permute-start.1 = (f32[]{:T(128)}, f32[]{:T(128)}, u32[]{:S(2)}, u32[]{:S(2)}) collective-permute-start(f32[]{:T(128)} %add.108), channel_id=1, source_target_pairs={{0,2},{1,3},{2,0},{3,1},{4,6},{5,7},{6,4},{7,5},{8,10},{9,11},{10,... | collective-permute-start | bytes 20 | tf_op jit(solution)/shard_map/ppermute | solution.py:92
  366.7 5.4 %collective-permute-start.5 = (f32[]{:T(128)}, f32[]{:T(128)}, u32[]{:S(2)}, u32[]{:S(2)}) collective-permute-start(f32[]{:T(128)} %add.112), channel_id=1, source_target_pairs={{0,2},{1,3},{2,0},{3,1},{4,6},{5,7},{6,4},{7,5},{8,10},{9,11},{10,... | collective-permute-start | bytes 20 | tf_op jit(solution)/shard_map/ppermute | solution.py:92
  369.4 5.4 %collective-permute-start.2 = (f32[]{:T(128)}, f32[]{:T(128)}, u32[]{:S(2)}, u32[]{:S(2)}) collective-permute-start(f32[]{:T(128)} %add.109), channel_id=1, source_target_pairs={{0,4},{1,5},{2,6},{3,7},{4,0},{5,1},{6,2},{7,3},{8,12},{9,13},{10,... | collective-permute-start | bytes 20 | tf_op jit(solution)/shard_map/ppermute | solution.py:92
  372.7 5.5 %collective-permute-start.6 = (f32[]{:T(128)}, f32[]{:T(128)}, u32[]{:S(2)}, u32[]{:S(2)}) collective-permute-start(f32[]{:T(128)} %add.113), channel_id=1, source_target_pairs={{0,4},{1,5},{2,6},{3,7},{4,0},{5,1},{6,2},{7,3},{8,12},{9,13},{10,... | collective-permute-start | bytes 20 | tf_op jit(solution)/shard_map/ppermute | solution.py:92
  375.4 6.3 %collective-permute-start.3 = (f32[]{:T(128)}, f32[]{:T(128)}, u32[]{:S(2)}, u32[]{:S(2)}) collective-permute-start(f32[]{:T(128)} %add.110), channel_id=1, source_target_pairs={{0,8},{1,9},{2,10},{3,11},{4,12},{5,13},{6,14},{7,15},{8,0},{9,1},... | collective-permute-start | bytes 20 | tf_op jit(solution)/shard_map/ppermute | solution.py:92
  378.8 4.5 %collective-permute-start.7 = (f32[]{:T(128)}, f32[]{:T(128)}, u32[]{:S(2)}, u32[]{:S(2)}) collective-permute-start(f32[]{:T(128)} %add.114), channel_id=1, source_target_pairs={{0,8},{1,9},{2,10},{3,11},{4,12},{5,13},{6,14},{7,15},{8,0},{9,1},... | collective-permute-start | bytes 20 | tf_op jit(solution)/shard_map/ppermute | solution.py:92
Sparse Core Ops, SparseCore 0:
  10.7 39.4 all-gather.4
  68.0 56.9 reduce-scatter.3
  127.9 35.7 all-gather.6
  183.2 56.9 reduce-scatter.5
  242.7 35.7 all-gather.8
  298.0 56.8 reduce-scatter.7
  357.9 35.7 all-gather.10
